TPU v7x, 32 devices: a whole 2x2x4 slice. The times are simulated.
32 devices in a mesh: tg: 4 (over y, x), fft: 8 (over z, core).
Axes of the slice: x: 2, y: 2, z: 4, core: 2. Of those that a mesh axis runs over, the one named last changes fastest.
Arguments:
- coeffs: float32 [4, 2, 240, 2048], P(None, None, None, ('tg', 'fft')), may hold values from -6 to 6
- stick_count: int32 [32], replicated, may hold values from 16 to 64, as said below
- stick_column: int32 [2048], replicated, may hold values from 0 to 57599, as said below
- plane_owner: int32 [240], replicated, may hold values from 0 to 7, as said below
- potential: float32 [240, 57600], P('fft'), may hold values from -3 to 1
Outputs:
- applied: float32 [4, 2, 240, 2048], P(None, None, None, ('tg', 'fft'))
Inputs may be any that keep to these rules, and one draw needn't show every extreme that they name: `stick_count`: each block of 64 slots holds at least 16 live sticks; max(1, 4 * 8 // 8) blocks are full in every draw. `stick_column`: all entries are distinct. `plane_owner`: no fft index owns more than 30 planes, and some own exactly 30.
All inputs are finite; a program needn't handle non-finite values.
Results may differ from a plain program's by a relative error of at most 0.000071.
Values sent between devices are 32-bit elements; how exact they have to be, the bound alone decides.
A program may use at most 256 MiB of HBM per device.

v0:
```python
import functools
import math

import jax
import jax.numpy as jnp
import ml_dtypes
import numpy as np
from jax import lax
from jax.experimental import pallas as pl
from jax.experimental.pallas import tpu as pltpu
from jax.sharding import PartitionSpec as P

NX = 240
NY = 240
NZ = 240
PAD = 256
HALF_X = NX // 2
SLOTS = 8
HIGHEST = lax.Precision.HIGHEST
HIGH = lax.Precision.HIGH


def cos_sin(length):
    indices = np.arange(length)
    angles = (indices[:, None] * indices[None, :] % length) * (2.0 * math.pi / length)
    factor = 1.0 / math.sqrt(length)
    return np.cos(angles) * factor, np.sin(angles) * factor


def split_table():
    cos_part, sin_part = cos_sin(NY)
    table = np.zeros((PAD, 2 * PAD), np.float32)
    table[:NY, :NY] = cos_part
    table[:NY, PAD : PAD + NY] = sin_part
    high = table.astype(ml_dtypes.bfloat16)
    low = (table - high.astype(np.float32)).astype(ml_dtypes.bfloat16)
    return high, low


def halves(values):
    high = values.astype(jnp.bfloat16)
    low = (values - high.astype(jnp.float32)).astype(jnp.bfloat16)
    return high, low


def dot(a, b):
    return jnp.dot(a, b, preferred_element_type=jnp.float32)


def grid_kernel(
    source_ref, row_ref, half_ref, sticks_ref, potential_ref, y_ref, x_ref, out_ref,
    columns, waves, staged,
):
    rows = sticks_ref.shape[0]
    stick_count = source_ref.shape[0]
    lane_half = lax.broadcasted_iota(jnp.int32, (1, 128), 1) // 64
    lanes = waves.shape[1] // PAD
    parts = lanes // 2

    def clear(i, carry):
        columns[pl.ds(pl.multiple_of(i * PAD, PAD), PAD), :] = jnp.zeros((PAD, 128), jnp.float32)
        return carry

    lax.fori_loop(0, HALF_X, clear, 0)
    staged[:rows, :] = sticks_ref[...]
    staged[rows:, :] = pltpu.roll(sticks_ref[...], 64, 1)

    def scatter(g, carry):
        value = staged[pl.ds(source_ref[g], 1), :]
        pltpu.store(columns.at[pl.ds(row_ref[g], 1), :], value, mask=lane_half == half_ref[g])
        return carry

    lax.fori_loop(0, stick_count, scatter, 0, unroll=8)
    waves[:, NX * lanes :, :] = jnp.zeros((2, (PAD - NX) * lanes, 128), jnp.float32)

    def load(at):
        return jnp.concatenate([waves[0, at, :], waves[1, at, :]], axis=1)

    def store(at, values):
        waves[0, at, :] = values[:, :128]
        waves[1, at, :] = values[:, 128:]

    def times_y(values):
        high, low = halves(values)
        total = dot(high, y_ref[0]) + dot(high, y_ref[1]) + dot(low, y_ref[0])
        return total.reshape(2, 2, parts, 2 * PAD)

    def forward_y(i, carry):
        block = columns[pl.ds(pl.multiple_of(i * PAD, PAD), PAD), :]
        total = times_y(block.T)
        real = total[:, 0, :, :PAD] - total[:, 1, :, PAD:]
        imag = total[:, 0, :, PAD:] + total[:, 1, :, :PAD]
        both = jnp.stack([real, imag], axis=1).reshape(128, PAD)
        store(pl.ds(pl.multiple_of(i * 128, 128), 128), both)
        return carry

    lax.fori_loop(0, HALF_X, forward_y, 0)

    def times_x(values):
        high, low = halves(values)
        total = dot(x_ref[0], high) + dot(x_ref[1], high) + dot(x_ref[0], low)
        return total[:PAD], total[PAD:]

    def planes(q, carry):
        at_real = pl.ds(q, PAD, stride=lanes)
        at_imag = pl.ds(q + parts, PAD, stride=lanes)
        cos_real, sin_real = times_x(load(at_real))
        cos_imag, sin_imag = times_x(load(at_imag))
        local = potential_ref[lax.rem(q, SLOTS)]
        real = (cos_real - sin_imag) * local
        imag = (sin_real + cos_imag) * local
        cos_real, sin_real = times_x(real)
        cos_imag, sin_imag = times_x(imag)
        store(at_real, cos_real + sin_imag)
        store(at_imag, cos_imag - sin_real)
        return carry

    lax.fori_loop(0, parts, planes, 0)

    def backward_y(i, carry):
        total = times_y(load(pl.ds(pl.multiple_of(i * 128, 128), 128)))
        real = total[:, 0, :, :PAD] + total[:, 1, :, PAD:]
        imag = total[:, 1, :, :PAD] - total[:, 0, :, PAD:]
        both = jnp.stack([real, imag], axis=1).reshape(128, PAD)
        columns[pl.ds(pl.multiple_of(i * PAD, PAD), PAD), :] = both.T
        return carry

    lax.fori_loop(0, HALF_X, backward_y, 0)
    staged[...] = jnp.zeros_like(staged)

    def gather(g, carry):
        value = columns[pl.ds(row_ref[g], 1), :]
        pltpu.store(staged.at[pl.ds(source_ref[g], 1), :], value, mask=lane_half == half_ref[g])
        return carry

    lax.fori_loop(0, stick_count, gather, 0, unroll=8)
    out_ref[...] = staged[:rows, :] + pltpu.roll(staged[rows:, :], 64, 1)


def on_grid(source, row, half, sticks, potential):
    rows = sticks.shape[0]
    high, low = split_table()
    y_table = jnp.asarray(np.stack([high, low]))
    x_table = jnp.asarray(np.stack([high.T, low.T]))
    smem = pl.BlockSpec(memory_space=pltpu.SMEM)
    vmem = pl.BlockSpec(memory_space=pltpu.VMEM)
    return pl.pallas_call(
        grid_kernel,
        out_shape=jax.ShapeDtypeStruct((rows, 128), jnp.float32),
        in_specs=[smem] * 3 + [vmem] * 4,
        out_specs=vmem,
        scratch_shapes=[
            pltpu.VMEM((HALF_X * PAD, 128), jnp.float32),
            pltpu.VMEM((2, PAD * 64, 128), jnp.float32),
            pltpu.VMEM((2 * rows, 128), jnp.float32),
        ],
        compiler_params=pltpu.CompilerParams(vmem_limit_bytes=60 * 2**20),
    )(source, row, half, sticks, potential, y_table, x_table)


def per_device(coeffs, stick_count, stick_column, plane_owner, potential):
    tg_size = lax.axis_size("tg")
    fft_size = lax.axis_size("fft")
    devices = tg_size * fft_size
    bands, _, _, slot_count = coeffs.shape
    plane_slots = potential.shape[0]
    pairs = slot_count // 2
    chunk = -(-plane_slots // tg_size)
    tg = lax.axis_index("tg")
    device = tg * fft_size + lax.axis_index("fft")

    slot = jnp.arange(slot_count, dtype=jnp.int32)
    live = (slot[None, :] < stick_count[:, None]).reshape(-1)
    x = stick_column // NY
    half = x % 2
    row = jnp.where(live, x // 2 * PAD + stick_column % NY, NY)
    glob = jnp.arange(devices * slot_count, dtype=jnp.int32)
    within = glob % slot_count
    source = glob // slot_count * pairs + within % pairs
    source = source + jnp.where(within // pairs != half, devices * pairs, 0)

    planes = jnp.arange(NZ, dtype=jnp.int32)
    same_owner = plane_owner[None, :] == plane_owner[:, None]
    earlier = planes[None, :] < planes[:, None]
    ranks = jnp.sum((same_owner & earlier).astype(jnp.int32), axis=1)
    group = ranks // chunk
    place = ranks - jnp.minimum(group * chunk, plane_slots - SLOTS)
    plane_rows = (group * fft_size + plane_owner) * SLOTS + place
    table_rows = jnp.arange(devices * SLOTS, dtype=jnp.int32)
    pick = (table_rows[:, None] == plane_rows[None, :]).astype(jnp.float32)
    cos_part, sin_part = cos_sin(NZ)
    tables = jnp.asarray(np.concatenate([cos_part, sin_part], axis=1).astype(np.float32))
    lift = jnp.dot(pick, tables, precision=HIGHEST).reshape(devices, SLOTS, 2, NZ)
    lift_cos, lift_sin = lift[:, :, 0], lift[:, :, 1]
    forward = jnp.stack([jnp.stack([lift_cos, lift_sin]), jnp.stack([-lift_sin, lift_cos])])
    backward = jnp.stack([jnp.stack([lift_cos, -lift_sin]), jnp.stack([lift_sin, lift_cos])])

    start = jnp.minimum(tg * chunk, plane_slots - SLOTS)
    local = lax.dynamic_slice(potential, (start, 0), (SLOTS, NX * NY)).reshape(SLOTS, NX, NY)
    local = jnp.pad(local, ((0, 0), (0, PAD - NX), (0, PAD - NY)))

    lifted = jnp.einsum(
        "bczhj,cdmpz->mjhdbp", coeffs.reshape(bands, 2, NZ, 2, pairs), forward, precision=HIGH
    ).reshape(devices, pairs, 128)
    received = lax.all_to_all(lifted, ("tg", "fft"), split_axis=0, concat_axis=0, tiled=True)
    worked = on_grid(source, row, half, received.reshape(devices * pairs, 128), local)
    returned = lax.all_to_all(
        worked.reshape(devices, pairs, 128), ("tg", "fft"), split_axis=0, concat_axis=0, tiled=True
    )
    applied = jnp.einsum(
        "mjhcbp,cdmpz->bdzhj",
        returned.reshape(devices, pairs, 2, 2, bands, SLOTS), backward, precision=HIGH,
    ).reshape(bands, 2, NZ, slot_count)
    return jnp.where(slot < stick_count[device], applied, 0.0)


def solution(mesh):
    in_specs = (P(None, None, None, ("tg", "fft")), P(), P(), P(), P("fft", None))
    out_specs = P(None, None, None, ("tg", "fft"))
    return jax.shard_map(
        per_device, mesh=mesh, in_specs=in_specs, out_specs=out_specs, check_vma=False
    )
```

profile of v0, /device:TPU:0, one launch (start us, length us, event | category | flops | bytes accessed | tf_op | source)
XLA Modules:
  0.0 238.1 jit_solution(9923998641852092317)
XLA Ops:
  0.0 0.0 copy-start
  0.0 0.9 convert_reduce_fusion
  0.9 0.7 subtract_add_fusion
  1.6 1.5 fusion.14
  3.1 0.4 reshape.42
  3.6 0.4 fusion.41
  4.1 0.9 fusion.12
  5.0 0.0 copy-done
  5.0 1.8 convolution_bitcast_fusion
  6.8 0.3 copy.41
  7.1 1.4 copy.42
  8.5 7.4 %all-to-all-start = ((f32[32,32,128]{2,1,0:T(8,128)}), f32[32,32,128]{2,1,0:T(8,128)}, u32[]{:S(2)}, u32[]{:S(2)}) async-start(f32[32,32,128]{2,1,0:T(8,128)} %copy.42), calls=%async_computation | async-start | bytes 1048576 | tf_op jit(solution)/shard_map/all_to_all | solution.py:205
  15.9 3.5 %constant_dynamic-slice_fusion = f32[8,57600]{1,0:T(8,128)} fusion(f32[30,57600]{1,0:T(8,128)} %param.12, s32[]{:T(128)S(6)} %select_n.70), kind=kLoop, calls=%fused_computation.75 | loop fusion | bytes 3686404 | tf_op jit(solution)/shard_map/dynamic_slice | solution.py:199
  19.4 0.0 copy-start.3
  19.4 3.5 %reshape.46 = f32[8,240,240]{2,1,0:T(8,128)S(1)} reshape(f32[8,57600]{1,0:T(8,128)} %constant_dynamic-slice_fusion) | data formatting | bytes 3686400 | tf_op jit(solution)/shard_map/reshape | solution.py:199
  22.9 0.0 copy-done.3
  22.9 0.0 copy-start.2
  22.9 0.1 iota_compare_fusion.3
  23.0 0.1 lt.74
  23.1 1.5 pad.4.potential_ref
  24.6 0.0 copy-done.2
  24.7 0.6 fusion.25
  25.3 7.0 %all-to-all-done = f32[32,32,128]{2,1,0:T(8,128)} async-done(((f32[32,32,128]{2,1,0:T(8,128)}), f32[32,32,128]{2,1,0:T(8,128)}, u32[]{:S(2)}, u32[]{:S(2)}) %all-to-all-start) | async-done | bytes 524320 | tf_op jit(solution)/shard_map/all_to_all | solution.py:205
  32.3 0.0 copy-start.1
  32.3 179.5 %shard_map.82 = f32[1024,128]{1,0:T(8,128)} custom-call(s32[2048]{0:T(1024)} %get-tuple-element.5.source_ref, s32[2048]{0:T(1024)} %get-tuple-element.15.row_ref, s32[2048]{0:T(1024)} %get-tuple-element.6.half_ref, f32[1024,128]{1,0:T(8,128)} %bitcast.17.sticks_ref, f32[8,256,256]{2,1,0:T(8,128)} %pad.4.potential_ref, ...), custom_call_target="tpu_custom_call" | custom-call | tf_op jit(solution)/shard_map/pallas_call | solution.py:147
  211.8 2.6 %all-to-all-start.1 = ((f32[32,32,128]{2,1,0:T(8,128)}), f32[32,32,128]{2,1,0:T(8,128)S(1)}, u32[]{:S(2)}, u32[]{:S(2)}) async-start(f32[32,32,128]{2,1,0:T(8,128)} %bitcast.58), calls=%async_computation.1 | async-start | bytes 1048576 | tf_op jit(solution)/shard_map/all_to_all | solution.py:207
  214.4 0.6 dynamic_slice.6
  215.0 0.6 iota_compare_fusion.4
  215.7 0.0 copy-done.1
  215.7 1.1 maximum_bitcast_fusion
  216.8 14.0 %all-to-all-done.1 = f32[32,32,128]{2,1,0:T(8,128)S(1)} async-done(((f32[32,32,128]{2,1,0:T(8,128)}), f32[32,32,128]{2,1,0:T(8,128)S(1)}, u32[]{:S(2)}, u32[]{:S(2)}) %all-to-all-start.1) | async-done | bytes 524320 | tf_op jit(solution)/shard_map/all_to_all | solution.py:207
  230.8 0.6 copy.43
  231.4 2.2 copy.45
  233.6 3.5 %fusion.2 = f32[4,2,240,2,32]{2,4,0,3,1:T(8,128)S(1)} fusion(f32[32,32,2,2,4,8]{0,1,5,3,4,2:T(8,128)} %copy.45, f32[2,2,32,8,240,1,1]{4,3,2,1,0,6,5:T(8,128)} %maximum_bitcast_fusion), kind=kOutput, calls=%fused_computation.3 | convolution fusion | flops 377487360 | bytes 1998848 | tf_op jit(solution)/shard_map/mjhcbp,cdmpz->bdzhj/dot_general | solution.py:210
  237.1 0.9 bitcast_select_fusion
  (3 shorter events, 0.1 us)
Async XLA Ops:
  0.0 5.0 %copy-start = (f32[4,2,240,64]{2,3,1,0:T(8,128)S(1)}, f32[4,2,240,64]{2,3,1,0:T(8,128)}, u32[]{:S(2)}) copy-start(f32[4,2,240,64]{2,3,1,0:T(8,128)} %param.8) | copy-start | bytes 1474564
  8.5 23.8 %all-to-all-start = ((f32[32,32,128]{2,1,0:T(8,128)}), f32[32,32,128]{2,1,0:T(8,128)}, u32[]{:S(2)}, u32[]{:S(2)}) async-start(f32[32,32,128]{2,1,0:T(8,128)} %copy.42), calls=%async_computation | async-start | bytes 1048576 | tf_op jit(solution)/shard_map/all_to_all | solution.py:205
  19.4 3.5 %copy-start.3 = (s32[32]{0:T(128)S(1)}, s32[32]{0:T(128)}, u32[]{:S(2)}) copy-start(s32[32]{0:T(128)} %param.9) | copy-start | bytes 388
  22.9 1.7 copy-start.2
  32.3 183.4 %copy-start.1 = (f32[1,2,32,8,240]{4,3,2,1,0:T(8,128)S(1)}, f32[1,2,32,8,240]{4,3,2,1,0:T(8,128)}, u32[]{:S(2)}) copy-start(f32[1,2,32,8,240]{4,3,2,1,0:T(8,128)} %get-tuple-element.14) | copy-start | bytes 1474564
  211.8 19.0 %all-to-all-start.1 = ((f32[32,32,128]{2,1,0:T(8,128)}), f32[32,32,128]{2,1,0:T(8,128)S(1)}, u32[]{:S(2)}, u32[]{:S(2)}) async-start(f32[32,32,128]{2,1,0:T(8,128)} %bitcast.58), calls=%async_computation.1 | async-start | bytes 1048576 | tf_op jit(solution)/shard_map/all_to_all | solution.py:207
where the time goes:
time: 238 us
  Pallas kernels  180 us (76%)
  waiting for transfers between devices  21 us (9%)
  local copies, waits for them, and re-layouts  14.7 us (6%)
  starting transfers between devices  10 us (4%)
  matrix products  6.82 us (3%)
  other arithmetic  5.88 us (2%)
    pallas_call x1, Pallas kernels, on_grid(): pl.pallas_call(grid_kernel, out_shape=jax.ShapeDtypeStruct((rows, 128), j...  180 us
    all_to_all x1, waiting for transfers between devices, per_device(): lax.all_to_all(worked.reshape(devices, pairs, 128), ('tg', 'fft'), split_...  14 us
    all_to_all x1, starting transfers between devices, per_device(): lax.all_to_all(lifted, ('tg', 'fft'), split_axis=0, concat_axis=0, tiled=...  7.43 us
    all_to_all x1, waiting for transfers between devices, per_device(): lax.all_to_all(lifted, ('tg', 'fft'), split_axis=0, concat_axis=0, tiled=...  6.98 us
  transfers between devices with their start and end apart: 2, of which 2 were waited for; matrix products, arithmetic and copies ran while one was open for 5% of the time, Pallas kernels for 0%

commit v1 on v0

--- a/solution.py
+++ b/solution.py
@@ -14,7 +14,12 @@
 NY = 240
 NZ = 240
 PAD = 256
-HALF_X = NX // 2
+FOLD = 128
+LANES = 64
+STRIDE = 72
+BLOCKS = 121
+UNROLL_Y = 11
+UNROLL_X = 4
 SLOTS = 8
 HIGHEST = lax.Precision.HIGHEST
 HIGH = lax.Precision.HIGH
@@ -27,14 +32,18 @@
     return np.cos(angles) * factor, np.sin(angles) * factor
 
 
-def split_table():
+def folded_table():
     cos_part, sin_part = cos_sin(NY)
-    table = np.zeros((PAD, 2 * PAD), np.float32)
-    table[:NY, :NY] = cos_part
-    table[:NY, PAD : PAD + NY] = sin_part
+    table = np.zeros((PAD, PAD), np.float32)
+    table[: NY // 2 + 1, :NY] = cos_part[: NY // 2 + 1]
+    table[FOLD : FOLD + NY // 2 + 1, :NY] = -sin_part[: NY // 2 + 1]
     high = table.astype(ml_dtypes.bfloat16)
     low = (table - high.astype(np.float32)).astype(ml_dtypes.bfloat16)
     return high, low
+
+
+def mirrored(index):
+    return jnp.where(index <= NY // 2, index, FOLD + NY - index)
 
 
 def halves(values):
@@ -48,20 +57,19 @@
 
 
 def grid_kernel(
-    source_ref, row_ref, half_ref, sticks_ref, potential_ref, y_ref, x_ref, out_ref,
+    source_ref, row_ref, half_ref, sticks_ref, potential_ref, table_ref, turned_ref, out_ref,
     columns, waves, staged,
 ):
     rows = sticks_ref.shape[0]
     stick_count = source_ref.shape[0]
     lane_half = lax.broadcasted_iota(jnp.int32, (1, 128), 1) // 64
-    lanes = waves.shape[1] // PAD
-    parts = lanes // 2
+    parts = LANES // 2
 
     def clear(i, carry):
         columns[pl.ds(pl.multiple_of(i * PAD, PAD), PAD), :] = jnp.zeros((PAD, 128), jnp.float32)
         return carry
 
-    lax.fori_loop(0, HALF_X, clear, 0)
+    lax.fori_loop(0, PAD // 2, clear, 0)
     staged[:rows, :] = sticks_ref[...]
     staged[rows:, :] = pltpu.roll(sticks_ref[...], 64, 1)
 
@@ -71,7 +79,8 @@
         return carry
 
     lax.fori_loop(0, stick_count, scatter, 0, unroll=8)
-    waves[:, NX * lanes :, :] = jnp.zeros((2, (PAD - NX) * lanes, 128), jnp.float32)
+    for first, last in ((122, 128), (248, 256)):
+        waves[:, first * STRIDE : last * STRIDE, :] = jnp.zeros((2, (last - first) * STRIDE, 128), jnp.float32)
 
     def load(at):
         return jnp.concatenate([waves[0, at, :], waves[1, at, :]], axis=1)
@@ -80,52 +89,70 @@
         waves[0, at, :] = values[:, :128]
         waves[1, at, :] = values[:, 128:]
 
-    def times_y(values):
+    def swapped(values):
+        grid = values.reshape(2, 2, parts, FOLD)
+        return grid[:, 0], grid[:, 1]
+
+    def joined(real, imag):
+        return jnp.stack([real, imag], axis=1).reshape(128, FOLD)
+
+    def block_of(i):
+        return i + jnp.where(i > 60, 3, 0)
+
+    def forward_y(i, carry):
+        block = block_of(i)
+        base = pl.multiple_of(block * PAD, PAD)
+        low_half = columns[pl.ds(base, FOLD), :]
+        high_half = columns[pl.ds(base + FOLD, FOLD), :]
+        even = (low_half + high_half).T
+        odd_real, odd_imag = swapped((low_half - high_half).T)
+        values = jnp.concatenate([even, joined(odd_imag, -odd_real)], axis=1)
         high, low = halves(values)
-        total = dot(high, y_ref[0]) + dot(high, y_ref[1]) + dot(low, y_ref[0])
-        return total.reshape(2, 2, parts, 2 * PAD)
-
-    def forward_y(i, carry):
-        block = columns[pl.ds(pl.multiple_of(i * PAD, PAD), PAD), :]
-        total = times_y(block.T)
-        real = total[:, 0, :, :PAD] - total[:, 1, :, PAD:]
-        imag = total[:, 0, :, PAD:] + total[:, 1, :, :PAD]
-        both = jnp.stack([real, imag], axis=1).reshape(128, PAD)
-        store(pl.ds(pl.multiple_of(i * 128, 128), 128), both)
-        return carry
-
-    lax.fori_loop(0, HALF_X, forward_y, 0)
-
-    def times_x(values):
+        total = dot(high, table_ref[0]) + dot(high, table_ref[1]) + dot(low, table_ref[0])
+        for h in range(2):
+            at = pl.ds(pl.multiple_of((block * 2 + h) * STRIDE, 8), LANES)
+            store(at, total[h * LANES : (h + 1) * LANES])
+        return carry
+
+    lax.fori_loop(0, BLOCKS, forward_y, 0, unroll=UNROLL_Y)
+
+    def three(table, values):
         high, low = halves(values)
-        total = dot(x_ref[0], high) + dot(x_ref[1], high) + dot(x_ref[0], low)
-        return total[:PAD], total[PAD:]
+        return dot(table[0], high) + dot(table[1], high) + dot(table[0], low)
 
     def planes(q, carry):
-        at_real = pl.ds(q, PAD, stride=lanes)
-        at_imag = pl.ds(q + parts, PAD, stride=lanes)
-        cos_real, sin_real = times_x(load(at_real))
-        cos_imag, sin_imag = times_x(load(at_imag))
+        at_real = pl.ds(q, PAD, stride=STRIDE)
+        at_imag = pl.ds(q + parts, PAD, stride=STRIDE)
+        real, imag = load(at_real), load(at_imag)
+        for_real = jnp.concatenate([real[:FOLD] + real[FOLD:], imag[:FOLD] - imag[FOLD:]])
+        for_imag = jnp.concatenate([imag[:FOLD] + imag[FOLD:], real[FOLD:] - real[:FOLD]])
         local = potential_ref[lax.rem(q, SLOTS)]
-        real = (cos_real - sin_imag) * local
-        imag = (sin_real + cos_imag) * local
-        cos_real, sin_real = times_x(real)
-        cos_imag, sin_imag = times_x(imag)
-        store(at_real, cos_real + sin_imag)
-        store(at_imag, cos_imag - sin_real)
-        return carry
-
-    lax.fori_loop(0, parts, planes, 0)
+        real = three(table=turned_ref, values=for_real) * local
+        imag = three(table=turned_ref, values=for_imag) * local
+        real = three(table_ref, real)
+        imag = three(table_ref, imag)
+        store(at_real, jnp.concatenate([real[:FOLD] - imag[FOLD:], real[:FOLD] + imag[FOLD:]]))
+        store(at_imag, jnp.concatenate([imag[:FOLD] + real[FOLD:], imag[:FOLD] - real[FOLD:]]))
+        return carry
+
+    lax.fori_loop(0, parts, planes, 0, unroll=UNROLL_X)
 
     def backward_y(i, carry):
-        total = times_y(load(pl.ds(pl.multiple_of(i * 128, 128), 128)))
-        real = total[:, 0, :, :PAD] + total[:, 1, :, PAD:]
-        imag = total[:, 1, :, :PAD] - total[:, 0, :, PAD:]
-        both = jnp.stack([real, imag], axis=1).reshape(128, PAD)
-        columns[pl.ds(pl.multiple_of(i * PAD, PAD), PAD), :] = both.T
-        return carry
-
-    lax.fori_loop(0, HALF_X, backward_y, 0)
+        block = block_of(i)
+        values = jnp.concatenate(
+            [load(pl.ds(pl.multiple_of((block * 2 + h) * STRIDE, 8), LANES)) for h in range(2)]
+        )
+        high, low = halves(values)
+        total = dot(high, turned_ref[0]) + dot(high, turned_ref[1]) + dot(low, turned_ref[0])
+        cosine = total[:, :FOLD]
+        sine_real, sine_imag = swapped(total[:, FOLD:])
+        sine = joined(sine_imag, -sine_real)
+        base = pl.multiple_of(block * PAD, PAD)
+        columns[pl.ds(base, FOLD), :] = (cosine - sine).T
+        columns[pl.ds(base + FOLD, FOLD), :] = (cosine + sine).T
+        return carry
+
+    lax.fori_loop(0, BLOCKS, backward_y, 0, unroll=UNROLL_Y)
     staged[...] = jnp.zeros_like(staged)
 
     def gather(g, carry):
@@ -139,9 +166,9 @@
 
 def on_grid(source, row, half, sticks, potential):
     rows = sticks.shape[0]
-    high, low = split_table()
-    y_table = jnp.asarray(np.stack([high, low]))
-    x_table = jnp.asarray(np.stack([high.T, low.T]))
+    high, low = folded_table()
+    table = jnp.asarray(np.stack([high, low]))
+    turned = jnp.asarray(np.stack([high.T, low.T]))
     smem = pl.BlockSpec(memory_space=pltpu.SMEM)
     vmem = pl.BlockSpec(memory_space=pltpu.VMEM)
     return pl.pallas_call(
@@ -150,12 +177,12 @@
         in_specs=[smem] * 3 + [vmem] * 4,
         out_specs=vmem,
         scratch_shapes=[
-            pltpu.VMEM((HALF_X * PAD, 128), jnp.float32),
-            pltpu.VMEM((2, PAD * 64, 128), jnp.float32),
+            pltpu.VMEM((PAD // 2 * PAD, 128), jnp.float32),
+            pltpu.VMEM((2, PAD * STRIDE, 128), jnp.float32),
             pltpu.VMEM((2 * rows, 128), jnp.float32),
         ],
         compiler_params=pltpu.CompilerParams(vmem_limit_bytes=60 * 2**20),
-    )(source, row, half, sticks, potential, y_table, x_table)
+    )(source, row, half, sticks, potential, table, turned)
 
 
 def per_device(coeffs, stick_count, stick_column, plane_owner, potential):
@@ -171,9 +198,9 @@
 
     slot = jnp.arange(slot_count, dtype=jnp.int32)
     live = (slot[None, :] < stick_count[:, None]).reshape(-1)
-    x = stick_column // NY
+    x = mirrored(stick_column // NY)
     half = x % 2
-    row = jnp.where(live, x // 2 * PAD + stick_column % NY, NY)
+    row = jnp.where(live, x // 2 * PAD + mirrored(stick_column % NY), NY // 2 + 1)
     glob = jnp.arange(devices * slot_count, dtype=jnp.int32)
     within = glob % slot_count
     source = glob // slot_count * pairs + within % pairs

time: 238 us -> 117 us (0.49)
  Pallas kernels: 180 us -> 57.5 us
    pallas_call x1, Pallas kernels: 180 us -> 57.5 us  [on_grid(): pl.pallas_call(grid_kernel, out_shape=jax.ShapeDtypeStruct((rows, 128), j...]
  transfers between devices with their start and end apart: 2 -> 2, of which waited for: 2 -> 2; matrix products, arithmetic and copies ran while one was open for 5% -> 10% of each run, Pallas kernels for 0% -> 0%
where the time goes in v1:
time: 117 us
  Pallas kernels  57.5 us (49%)
  waiting for transfers between devices  20.8 us (18%)
  local copies, waits for them, and re-layouts  15.4 us (13%)
  starting transfers between devices  10.1 us (9%)
  matrix products  6.82 us (6%)
  other arithmetic  5.89 us (5%)
    pallas_call x1, Pallas kernels, on_grid(): pl.pallas_call(grid_kernel, out_shape=jax.ShapeDtypeStruct((rows, 128), j...  57.5 us
    all_to_all x1, waiting for transfers between devices, per_device(): lax.all_to_all(worked.reshape(devices, pairs, 128), ('tg', 'fft'), split_...  13.8 us
    all_to_all x1, starting transfers between devices, per_device(): lax.all_to_all(lifted, ('tg', 'fft'), split_axis=0, concat_axis=0, tiled=...  7.3 us
    all_to_all x1, waiting for transfers between devices, per_device(): lax.all_to_all(lifted, ('tg', 'fft'), split_axis=0, concat_axis=0, tiled=...  7.02 us
    dot_general x1, matrix products, per_device(): jnp.einsum('mjhcbp,cdmpz->bdzhj', returned.reshape(devices, pairs, 2, 2,...  3.54 us
    dynamic_slice x1, local copies, waits for them, and re-layouts, per_device(): lax.dynamic_slice(potential, (start, 0), (SLOTS, NX * NY))  3.49 us
    reshape x1, local copies, waits for them, and re-layouts, per_device(): lax.dynamic_slice(potential, (start, 0), (SLOTS, NX * NY))  3.47 us
    all_to_all x1, starting transfers between devices, per_device(): lax.all_to_all(worked.reshape(devices, pairs, 128), ('tg', 'fft'), split_...  2.78 us
  transfers between devices with their start and end apart: 2, of which 2 were waited for; matrix products, arithmetic and copies ran while one was open for 10% of the time, Pallas kernels for 0%

profile of v1, /device:TPU:0, one launch (start us, length us, event | category | flops | bytes accessed | tf_op | source)
XLA Modules:
  0.0 116.7 jit_solution(460898502879307921)
XLA Ops:
  0.0 0.0 copy-start
  0.0 0.9 convert_reduce_fusion
  0.9 0.7 subtract_add_fusion
  1.6 1.5 %fusion.14 = f32[256,480]{1,0:T(8,128)S(1)} fusion(f32[240,480]{1,0:T(8,128)} %constant.130.clone, s32[240]{0:T(256)S(1)} %subtract_add_fusion), kind=kOutput, calls=%fused_computation.22 | convolution fusion | flops 353955840 | bytes 953280 | tf_op jit(solution)/shard_map/dot_general | solution.py:220
  3.1 0.4 reshape.42
  3.6 0.4 fusion.41
  4.1 0.9 fusion.12
  5.0 0.0 copy-done
  5.0 1.8 %convolution_bitcast_fusion = f32[32,32,2,2,4,8]{1,5,2,4,0,3:T(8,128)S(1)} fusion(f32[4,2,240,2,32,1,1]{2,4,3,1,0,6,5:T(8,128)S(1)} %bitcast.55, f32[1,2,32,8,240]{4,3,0,2,1:T(8,128)S(1)} %get-tuple-element.8, f32[1,2,32,8,240]{4,3,0,2,1:T(8,128)S(1)} %get-tuple-element.13), kind=kOutput, calls=%fused_computation.2 | convolution fusion | flops 377733120 | bytes 1998848 | tf_op jit(solution)/shard_map/bczhj,cdmpz->mjhdbp/dot_general | solution.py:229
  6.8 0.3 copy.41
  7.1 1.4 %copy.42 = f32[32,32,128]{2,1,0:T(8,128)} copy(f32[32,32,128]{1,2,0:T(8,128)S(1)} %bitcast.56) | data formatting | bytes 1048576 | tf_op jit(solution)/shard_map/reshape | solution.py:231
  8.5 7.3 %all-to-all-start = ((f32[32,32,128]{2,1,0:T(8,128)}), f32[32,32,128]{2,1,0:T(8,128)S(1)}, u32[]{:S(2)}, u32[]{:S(2)}) async-start(f32[32,32,128]{2,1,0:T(8,128)} %copy.42), calls=%async_computation | async-start | bytes 1048576 | tf_op jit(solution)/shard_map/all_to_all | solution.py:232
  15.8 3.5 %constant_dynamic-slice_fusion = f32[8,57600]{1,0:T(8,128)} fusion(f32[30,57600]{1,0:T(8,128)} %param.12, s32[]{:T(128)S(6)} %select_n.78), kind=kLoop, calls=%fused_computation.77 | loop fusion | bytes 3686404 | tf_op jit(solution)/shard_map/dynamic_slice | solution.py:226
  19.3 0.0 copy-start.4
  19.3 3.5 %reshape.46 = f32[8,240,240]{2,1,0:T(8,128)S(1)} reshape(f32[8,57600]{1,0:T(8,128)} %constant_dynamic-slice_fusion) | data formatting | bytes 3686400 | tf_op jit(solution)/shard_map/reshape | solution.py:226
  22.8 0.0 copy-done.4
  22.8 0.0 copy-start.3
  22.8 0.1 iota_compare_fusion.3
  22.9 0.1 lt.74
  23.0 1.5 %pad.4.potential_ref = f32[8,256,256]{2,1,0:T(8,128)} pad(f32[8,240,240]{2,1,0:T(8,128)S(1)} %reshape.46, f32[]{:T(128)} %constant.129.clone.1), padding=0_0x0_16x0_16 | pad | bytes 3940356 | tf_op jit(solution)/shard_map/jit(_pad)/pad | solution.py:227
  24.5 0.0 copy-done.3
  24.5 0.6 fusion.25
  25.1 7.0 %all-to-all-done = f32[32,32,128]{2,1,0:T(8,128)S(1)} async-done(((f32[32,32,128]{2,1,0:T(8,128)}), f32[32,32,128]{2,1,0:T(8,128)S(1)}, u32[]{:S(2)}, u32[]{:S(2)}) %all-to-all-start) | async-done | bytes 524320 | tf_op jit(solution)/shard_map/all_to_all | solution.py:232
  32.1 0.0 copy-start.1
  32.1 0.8 copy-done.1
  32.9 0.0 copy-start.5
  32.9 0.0 copy-start.2
  32.9 57.5 %shard_map.82 = f32[1024,128]{1,0:T(8,128)} custom-call(s32[2048]{0:T(1024)} %get-tuple-element.5.source_ref, s32[2048]{0:T(1024)} %get-tuple-element.15.row_ref, s32[2048]{0:T(1024)} %get-tuple-element.6.half_ref, f32[1024,128]{1,0:T(8,128)} %bitcast.58, f32[8,256,256]{2,1,0:T(8,128)} %pad.4.potential_ref, bf16[2,256,256]{2,1,0:T(8,128)(2,1)} %constant.131.clone.table_ref, ...), custom_call_target="tpu_custom_call" | custom-call | tf_op jit(solution)/shard_map/pallas_call | solution.py:174
  90.5 2.8 %all-to-all-start.1 = ((f32[32,32,128]{2,1,0:T(8,128)}), f32[32,32,128]{2,1,0:T(8,128)S(1)}, u32[]{:S(2)}, u32[]{:S(2)}) async-start(f32[32,32,128]{2,1,0:T(8,128)} %bitcast.59), calls=%async_computation.1 | async-start | bytes 1048576 | tf_op jit(solution)/shard_map/all_to_all | solution.py:234
  93.3 0.0 copy-done.5
  93.3 0.7 dynamic_slice.6
  93.9 0.6 iota_compare_fusion.4
  94.6 0.0 copy-done.2
  94.6 1.1 maximum_bitcast_fusion
  95.7 13.8 %all-to-all-done.1 = f32[32,32,128]{2,1,0:T(8,128)S(1)} async-done(((f32[32,32,128]{2,1,0:T(8,128)}), f32[32,32,128]{2,1,0:T(8,128)S(1)}, u32[]{:S(2)}, u32[]{:S(2)}) %all-to-all-start.1) | async-done | bytes 524320 | tf_op jit(solution)/shard_map/all_to_all | solution.py:234
  109.4 0.6 copy.43
  110.1 2.2 %copy.45 = f32[32,32,2,2,4,8]{0,1,5,3,4,2:T(8,128)} copy(f32[32,32,2,2,4,8]{1,5,4,3,2,0:T(8,128)S(1)} %bitcast.57) | data formatting | bytes 1048576 | tf_op jit(solution)/shard_map/reshape | solution.py:239
  112.2 3.5 %fusion.2 = f32[4,2,240,2,32]{2,4,0,3,1:T(8,128)S(1)} fusion(f32[32,32,2,2,4,8]{0,1,5,3,4,2:T(8,128)} %copy.45, f32[2,2,32,8,240,1,1]{4,3,2,1,0,6,5:T(8,128)} %maximum_bitcast_fusion), kind=kOutput, calls=%fused_computation.3 | convolution fusion | flops 377487360 | bytes 1998848 | tf_op jit(solution)/shard_map/mjhcbp,cdmpz->bdzhj/dot_general | solution.py:237
  115.8 0.9 bitcast_select_fusion
  (3 shorter events, 0.1 us)
Async XLA Ops:
  0.0 5.0 %copy-start = (f32[4,2,240,64]{2,3,1,0:T(8,128)S(1)}, f32[4,2,240,64]{2,3,1,0:T(8,128)}, u32[]{:S(2)}) copy-start(f32[4,2,240,64]{2,3,1,0:T(8,128)} %param.8) | copy-start | bytes 1474564
  8.5 23.7 %all-to-all-start = ((f32[32,32,128]{2,1,0:T(8,128)}), f32[32,32,128]{2,1,0:T(8,128)S(1)}, u32[]{:S(2)}, u32[]{:S(2)}) async-start(f32[32,32,128]{2,1,0:T(8,128)} %copy.42), calls=%async_computation | async-start | bytes 1048576 | tf_op jit(solution)/shard_map/all_to_all | solution.py:232
  19.3 3.5 %copy-start.4 = (s32[32]{0:T(128)S(1)}, s32[32]{0:T(128)}, u32[]{:S(2)}) copy-start(s32[32]{0:T(128)} %param.9) | copy-start | bytes 388
  22.8 1.7 %copy-start.3 = (s32[2048]{0:T(1024)S(1)}, s32[2048]{0:T(1024)}, u32[]{:S(2)}) copy-start(s32[2048]{0:T(1024)} %param.10) | copy-start | bytes 24580
  32.1 0.8 copy-start.1
  32.9 60.4 %copy-start.5 = (s32[32]{0:T(128)S(1)}, s32[32]{0:T(128)}, u32[]{:S(2)}) copy-start(s32[32]{0:T(128)} %param.9) | copy-start | bytes 388
  32.9 61.6 %copy-start.2 = (f32[1,2,32,8,240]{4,3,2,1,0:T(8,128)S(1)}, f32[1,2,32,8,240]{4,3,2,1,0:T(8,128)}, u32[]{:S(2)}) copy-start(f32[1,2,32,8,240]{4,3,2,1,0:T(8,128)} %get-tuple-element.14) | copy-start | bytes 1474564
  90.5 19.0 %all-to-all-start.1 = ((f32[32,32,128]{2,1,0:T(8,128)}), f32[32,32,128]{2,1,0:T(8,128)S(1)}, u32[]{:S(2)}, u32[]{:S(2)}) async-start(f32[32,32,128]{2,1,0:T(8,128)} %bitcast.59), calls=%async_computation.1 | async-start | bytes 1048576 | tf_op jit(solution)/shard_map/all_to_all | solution.py:234

commit v2 on v1

--- a/solution.py
+++ b/solution.py
@@ -19,7 +19,8 @@
 STRIDE = 72
 BLOCKS = 121
 UNROLL_Y = 11
-UNROLL_X = 4
+UNROLL_G = 32
+UNROLL_X = 8
 SLOTS = 8
 HIGHEST = lax.Precision.HIGHEST
 HIGH = lax.Precision.HIGH
@@ -78,7 +79,7 @@
         pltpu.store(columns.at[pl.ds(row_ref[g], 1), :], value, mask=lane_half == half_ref[g])
         return carry
 
-    lax.fori_loop(0, stick_count, scatter, 0, unroll=8)
+    lax.fori_loop(0, stick_count, scatter, 0, unroll=UNROLL_G)
     for first, last in ((122, 128), (248, 256)):
         waves[:, first * STRIDE : last * STRIDE, :] = jnp.zeros((2, (last - first) * STRIDE, 128), jnp.float32)
 
@@ -160,7 +161,7 @@
         pltpu.store(staged.at[pl.ds(source_ref[g], 1), :], value, mask=lane_half == half_ref[g])
         return carry
 
-    lax.fori_loop(0, stick_count, gather, 0, unroll=8)
+    lax.fori_loop(0, stick_count, gather, 0, unroll=UNROLL_G)
     out_ref[...] = staged[:rows, :] + pltpu.roll(staged[rows:, :], 64, 1)
 
 

time: 117 us -> 115 us (0.983)
  Pallas kernels: 57.5 us -> 55.1 us
    pallas_call x1, Pallas kernels: 57.5 us -> 55.1 us  [on_grid(): pl.pallas_call(grid_kernel, out_shape=jax.ShapeDtypeStruct((rows, 128), j...]
where the time goes in v2:
time: 115 us; the launch traced here: 114 us
  Pallas kernels  55.1 us (48%)
  waiting for transfers between devices  20.8 us (18%)
  local copies, waits for them, and re-layouts  15.4 us (13%)
  starting transfers between devices  10.1 us (9%)
  matrix products  6.82 us (6%)
  other arithmetic  5.89 us (5%)
    pallas_call x1, Pallas kernels, on_grid(): pl.pallas_call(grid_kernel, out_shape=jax.ShapeDtypeStruct((rows, 128), j...  55.1 us
    all_to_all x1, waiting for transfers between devices, per_device(): lax.all_to_all(worked.reshape(devices, pairs, 128), ('tg', 'fft'), split_...  14 us
    all_to_all x1, starting transfers between devices, per_device(): lax.all_to_all(lifted, ('tg', 'fft'), split_axis=0, concat_axis=0, tiled=...  7.48 us
    all_to_all x1, waiting for transfers between devices, per_device(): lax.all_to_all(lifted, ('tg', 'fft'), split_axis=0, concat_axis=0, tiled=...  6.84 us
    dot_general x1, matrix products, per_device(): jnp.einsum('mjhcbp,cdmpz->bdzhj', returned.reshape(devices, pairs, 2, 2,...  3.54 us
    dynamic_slice x1, local copies, waits for them, and re-layouts, per_device(): lax.dynamic_slice(potential, (start, 0), (SLOTS, NX * NY))  3.49 us
    reshape x1, local copies, waits for them, and re-layouts, per_device(): lax.dynamic_slice(potential, (start, 0), (SLOTS, NX * NY))  3.47 us
    all_to_all x1, starting transfers between devices, per_device(): lax.all_to_all(worked.reshape(devices, pairs, 128), ('tg', 'fft'), split_...  2.6 us
  transfers between devices with their start and end apart: 2, of which 2 were waited for; matrix products, arithmetic and copies ran while one was open for 10% of the time, Pallas kernels for 0%

profile of v2, /device:TPU:0, one launch (start us, length us, event | category | flops | bytes accessed | tf_op | source)
XLA Modules:
  0.0 114.3 jit_solution(8714141582436640424)
XLA Ops:
  0.0 0.0 copy-start
  0.0 0.9 convert_reduce_fusion
  0.9 0.7 subtract_add_fusion
  1.6 1.5 %fusion.14 = f32[256,480]{1,0:T(8,128)S(1)} fusion(f32[240,480]{1,0:T(8,128)} %constant.130.clone, s32[240]{0:T(256)S(1)} %subtract_add_fusion), kind=kOutput, calls=%fused_computation.22 | convolution fusion | flops 353955840 | bytes 953280 | tf_op jit(solution)/shard_map/dot_general | solution.py:221
  3.1 0.4 reshape.42
  3.6 0.4 fusion.41
  4.1 0.9 fusion.12
  5.0 0.0 copy-done
  5.0 1.8 %convolution_bitcast_fusion = f32[32,32,2,2,4,8]{1,5,2,4,0,3:T(8,128)S(1)} fusion(f32[4,2,240,2,32,1,1]{2,4,3,1,0,6,5:T(8,128)S(1)} %bitcast.55, f32[1,2,32,8,240]{4,3,0,2,1:T(8,128)S(1)} %get-tuple-element.8, f32[1,2,32,8,240]{4,3,0,2,1:T(8,128)S(1)} %get-tuple-element.13), kind=kOutput, calls=%fused_computation.2 | convolution fusion | flops 377733120 | bytes 1998848 | tf_op jit(solution)/shard_map/bczhj,cdmpz->mjhdbp/dot_general | solution.py:230
  6.8 0.3 copy.41
  7.1 1.4 %copy.42 = f32[32,32,128]{2,1,0:T(8,128)} copy(f32[32,32,128]{1,2,0:T(8,128)S(1)} %bitcast.56) | data formatting | bytes 1048576 | tf_op jit(solution)/shard_map/reshape | solution.py:232
  8.5 7.5 %all-to-all-start = ((f32[32,32,128]{2,1,0:T(8,128)}), f32[32,32,128]{2,1,0:T(8,128)S(1)}, u32[]{:S(2)}, u32[]{:S(2)}) async-start(f32[32,32,128]{2,1,0:T(8,128)} %copy.42), calls=%async_computation | async-start | bytes 1048576 | tf_op jit(solution)/shard_map/all_to_all | solution.py:233
  16.0 3.5 %constant_dynamic-slice_fusion = f32[8,57600]{1,0:T(8,128)} fusion(f32[30,57600]{1,0:T(8,128)} %param.12, s32[]{:T(128)S(6)} %select_n.78), kind=kLoop, calls=%fused_computation.77 | loop fusion | bytes 3686404 | tf_op jit(solution)/shard_map/dynamic_slice | solution.py:227
  19.5 0.0 copy-start.4
  19.5 3.5 %reshape.46 = f32[8,240,240]{2,1,0:T(8,128)S(1)} reshape(f32[8,57600]{1,0:T(8,128)} %constant_dynamic-slice_fusion) | data formatting | bytes 3686400 | tf_op jit(solution)/shard_map/reshape | solution.py:227
  22.9 0.0 copy-done.4
  23.0 0.0 copy-start.3
  23.0 0.1 iota_compare_fusion.3
  23.0 0.1 lt.74
  23.1 1.5 %pad.4.potential_ref = f32[8,256,256]{2,1,0:T(8,128)} pad(f32[8,240,240]{2,1,0:T(8,128)S(1)} %reshape.46, f32[]{:T(128)} %constant.129.clone.1), padding=0_0x0_16x0_16 | pad | bytes 3940356 | tf_op jit(solution)/shard_map/jit(_pad)/pad | solution.py:228
  24.7 0.0 copy-done.3
  24.7 0.6 fusion.25
  25.3 6.8 %all-to-all-done = f32[32,32,128]{2,1,0:T(8,128)S(1)} async-done(((f32[32,32,128]{2,1,0:T(8,128)}), f32[32,32,128]{2,1,0:T(8,128)S(1)}, u32[]{:S(2)}, u32[]{:S(2)}) %all-to-all-start) | async-done | bytes 524320 | tf_op jit(solution)/shard_map/all_to_all | solution.py:233
  32.1 0.0 copy-start.1
  32.1 0.8 copy-done.1
  32.9 0.0 copy-start.5
  32.9 0.0 copy-start.2
  32.9 55.1 %shard_map.82 = f32[1024,128]{1,0:T(8,128)} custom-call(s32[2048]{0:T(1024)} %get-tuple-element.5.source_ref, s32[2048]{0:T(1024)} %get-tuple-element.15.row_ref, s32[2048]{0:T(1024)} %get-tuple-element.6.half_ref, f32[1024,128]{1,0:T(8,128)} %bitcast.58, f32[8,256,256]{2,1,0:T(8,128)} %pad.4.potential_ref, bf16[2,256,256]{2,1,0:T(8,128)(2,1)} %constant.131.clone.table_ref, ...), custom_call_target="tpu_custom_call" | custom-call | tf_op jit(solution)/shard_map/pallas_call | solution.py:175
  88.0 2.6 %all-to-all-start.1 = ((f32[32,32,128]{2,1,0:T(8,128)}), f32[32,32,128]{2,1,0:T(8,128)S(1)}, u32[]{:S(2)}, u32[]{:S(2)}) async-start(f32[32,32,128]{2,1,0:T(8,128)} %bitcast.59), calls=%async_computation.1 | async-start | bytes 1048576 | tf_op jit(solution)/shard_map/all_to_all | solution.py:235
  90.6 0.0 copy-done.5
  90.7 0.7 dynamic_slice.6
  91.3 0.6 iota_compare_fusion.4
  91.9 0.0 copy-done.2
  91.9 1.1 maximum_bitcast_fusion
  93.0 14.0 %all-to-all-done.1 = f32[32,32,128]{2,1,0:T(8,128)S(1)} async-done(((f32[32,32,128]{2,1,0:T(8,128)}), f32[32,32,128]{2,1,0:T(8,128)S(1)}, u32[]{:S(2)}, u32[]{:S(2)}) %all-to-all-start.1) | async-done | bytes 524320 | tf_op jit(solution)/shard_map/all_to_all | solution.py:235
  107.0 0.6 copy.43
  107.6 2.2 %copy.45 = f32[32,32,2,2,4,8]{0,1,5,3,4,2:T(8,128)} copy(f32[32,32,2,2,4,8]{1,5,4,3,2,0:T(8,128)S(1)} %bitcast.57) | data formatting | bytes 1048576 | tf_op jit(solution)/shard_map/reshape | solution.py:240
  109.8 3.5 %fusion.2 = f32[4,2,240,2,32]{2,4,0,3,1:T(8,128)S(1)} fusion(f32[32,32,2,2,4,8]{0,1,5,3,4,2:T(8,128)} %copy.45, f32[2,2,32,8,240,1,1]{4,3,2,1,0,6,5:T(8,128)} %maximum_bitcast_fusion), kind=kOutput, calls=%fused_computation.3 | convolution fusion | flops 377487360 | bytes 1998848 | tf_op jit(solution)/shard_map/mjhcbp,cdmpz->bdzhj/dot_general | solution.py:238
  113.4 0.9 bitcast_select_fusion
  (3 shorter events, 0.1 us)
Async XLA Ops:
  0.0 5.0 %copy-start = (f32[4,2,240,64]{2,3,1,0:T(8,128)S(1)}, f32[4,2,240,64]{2,3,1,0:T(8,128)}, u32[]{:S(2)}) copy-start(f32[4,2,240,64]{2,3,1,0:T(8,128)} %param.8) | copy-start | bytes 1474564
  8.5 23.7 %all-to-all-start = ((f32[32,32,128]{2,1,0:T(8,128)}), f32[32,32,128]{2,1,0:T(8,128)S(1)}, u32[]{:S(2)}, u32[]{:S(2)}) async-start(f32[32,32,128]{2,1,0:T(8,128)} %copy.42), calls=%async_computation | async-start | bytes 1048576 | tf_op jit(solution)/shard_map/all_to_all | solution.py:233
  19.5 3.5 %copy-start.4 = (s32[32]{0:T(128)S(1)}, s32[32]{0:T(128)}, u32[]{:S(2)}) copy-start(s32[32]{0:T(128)} %param.9) | copy-start | bytes 388
  23.0 1.7 %copy-start.3 = (s32[2048]{0:T(1024)S(1)}, s32[2048]{0:T(1024)}, u32[]{:S(2)}) copy-start(s32[2048]{0:T(1024)} %param.10) | copy-start | bytes 24580
  32.1 0.8 copy-start.1
  32.9 57.7 %copy-start.5 = (s32[32]{0:T(128)S(1)}, s32[32]{0:T(128)}, u32[]{:S(2)}) copy-start(s32[32]{0:T(128)} %param.9) | copy-start | bytes 388
  32.9 59.0 %copy-start.2 = (f32[1,2,32,8,240]{4,3,2,1,0:T(8,128)S(1)}, f32[1,2,32,8,240]{4,3,2,1,0:T(8,128)}, u32[]{:S(2)}) copy-start(f32[1,2,32,8,240]{4,3,2,1,0:T(8,128)} %get-tuple-element.14) | copy-start | bytes 1474564
  88.0 19.0 %all-to-all-start.1 = ((f32[32,32,128]{2,1,0:T(8,128)}), f32[32,32,128]{2,1,0:T(8,128)S(1)}, u32[]{:S(2)}, u32[]{:S(2)}) async-start(f32[32,32,128]{2,1,0:T(8,128)} %bitcast.59), calls=%async_computation.1 | async-start | bytes 1048576 | tf_op jit(solution)/shard_map/all_to_all | solution.py:235
